TPU v7x, 128 devices: a whole 4x4x4 slice. The times are simulated.
128 devices in a mesh: leaf: 32 (over z, y, core), rows: 4 (over x).
Axes of the slice: x: 4, y: 4, z: 4, core: 2. Of those that a mesh axis runs over, the one named last changes fastest.
Arguments:
- child_update: float32 [32, 512, 512], P('leaf', 'rows'), as said below
- block_maps: int32 [3, 32, 4], replicated, may hold values from 0 to 11, as said below
- sep_share: float32 [32, 3, 1024, 1024], P('leaf', None, 'rows'), as said below
- coupling_share: float32 [32, 3, 512, 1024], P('leaf', None, 'rows')
Outputs:
- diag_factor: float32 [32, 3, 1024, 1024], P('leaf', None, 'rows')
- below_factor: float32 [32, 3, 512, 1024], P('leaf', None, 'rows')
- top_update: float32 [32, 512, 512], P('leaf', 'rows')
Inputs may be any that keep to these rules, and one draw needn't show every extreme that they name: Each row block_maps[k, c] names 4 different front blocks; at every level k, the rows 2g and 2g+1 together name every block from 8 on. At level k only the rows c < 32 / 2^k are used. `child_update`: Symmetric. `sep_share`: symmetric in its last two dimensions.
All inputs are finite; a program needn't handle non-finite values.
Results may differ from a plain program's by a relative error of at most 0.00012.
Values sent between devices are 32-bit elements; how exact they have to be, the bound alone decides.
No kernel may reach another device: no remote copies, remote signals or barrier semaphores. Data moves between devices by JAX's collectives and lax.ppermute only.
A program may use at most 192 MiB of HBM per device.

v0:
```python
import jax
import jax.numpy as jnp
from jax import lax
from jax.experimental import pallas as pl
from jax.experimental.pallas import tpu as pltpu
from jax.sharding import PartitionSpec as P

BLK = 128
SEP = 1024
UPD = 512
FRONT = SEP + UPD
LEVELS = 3
NSEP = SEP // BLK
NUPD = UPD // BLK
PART = 8
PAIR = 2 * BLK
CHUNK = 4
HALVES = (((0, 0), (1, 0), (1, 1), (2, 0), (2, 1)), ((2, 2), (3, 0), (3, 1), (3, 2), (3, 3)))
f32 = jnp.float32
bf16 = jnp.bfloat16


def lane_b(x, c):
    return jnp.broadcast_to(x[:, c : c + 1], x.shape)


def sub_b(x, i):
    return jnp.broadcast_to(x[i : i + 1, :], x.shape)


def block_inverse(rows_a):
    groups = BLK // 8
    row = lax.broadcasted_iota(jnp.int32, (8, BLK), 0)
    lane = lax.broadcasted_iota(jnp.int32, (8, BLK), 1)
    M = list(rows_a)
    out = []
    for s in range(0, groups, PART):
        e = s + PART
        cols = [lane_b(M[s], 8 * s + j) for j in range(8)]
        zrows = []
        for b in range(s, e):
            c0 = 8 * b
            inside = (lane >= c0) & (lane < c0 + 8)
            coef = {g: [lane_b(M[g], c0 + k) for k in range(8)] for g in range(b + 1, e)}
            following = [lane_b(M[b + 1], c0 + 8 + j) for j in range(8)] if b + 1 < e else None
            X = jnp.where(inside, jnp.where(lane - c0 == row, 1.0, 0.0), M[b])
            rs = []
            zs = []
            ls = [[None] * 8 for _ in range(8)]
            pivot = sub_b(cols[0], 0)
            for k in range(8):
                r = lax.rsqrt(pivot)
                rs.append(r)
                if k < 7:
                    below = sub_b(cols[k], k + 1) * r
                    pivot = sub_b(cols[k + 1], k + 1) - below * below
                c = cols[k] * r
                for j in range(k + 1, 8):
                    ls[j][k] = sub_b(c, j)
                    cols[j] = cols[j] - c * ls[j][k]
                z = sub_b(X, k) * r
                zs.append(z)
                if k < 7:
                    X = X - jnp.where(row > k, c, 0.0) * z
            for g in range(b + 1, e):
                cg = coef[g]
                for k in range(8):
                    cg[k] = cg[k] * rs[k]
                    for i in range(k + 1, 8):
                        cg[i] = cg[i] - ls[i][k] * cg[k]
                m = jnp.where(inside, 0.0, M[g])
                for k in range(8):
                    m = m - cg[k] * zs[k]
                M[g] = m
                if g == b + 1:
                    for k in range(8):
                        for j in range(8):
                            following[j] = following[j] - cg[k] * sub_b(cg[k], j)
                    cols = following
            y = zs[0]
            for k in range(1, 8):
                y = jnp.where(row == k, zs[k], y)
            zrows.append(jnp.where((lane < c0 + 8) | (lane >= 8 * e), y, 0.0))
            out.append(jnp.where(lane < c0 + 8, y, 0.0))
        if e < groups:
            zh, zl = split(jnp.concatenate(zrows, axis=0))
            lhs = jnp.concatenate([zh, zh, zl], axis=0)[:, 8 * e :]
            rhs = jnp.concatenate([zh, zl, zh], axis=0)
            upd = lax.dot_general(lhs, rhs, (((0,), (0,)), ((), ())), preferred_element_type=f32)
            done = (lane >= 8 * s) & (lane < 8 * e)
            for g in range(e, groups):
                M[g] = jnp.where(done, 0.0, M[g]) - upd[8 * (g - e) : 8 * (g - e) + 8, :]
    return out


def split(x):
    hi = x.astype(bf16)
    return hi, (x - hi.astype(f32)).astype(bf16)


def nt(a, b):
    return lax.dot_general(a, b, (((1,), (1,)), ((), ())), preferred_element_type=f32)


def stack_split(x):
    hi, lo = split(x)
    rows = x.shape[0] // BLK
    parts = []
    for i in range(rows):
        parts += [hi[i * BLK : (i + 1) * BLK], lo[i * BLK : (i + 1) * BLK]]
    return jnp.concatenate(parts, axis=0)


def nt4(a, b):
    p = nt(a, b)
    rows = []
    for i in range(a.shape[0] // PAIR):
        cols = []
        for j in range(b.shape[0] // PAIR):
            q = p[i * PAIR : (i + 1) * PAIR, j * PAIR : (j + 1) * PAIR]
            cols.append(q[:BLK, :BLK] + (q[:BLK, BLK:] + q[BLK:, :BLK]) + q[BLK:, BLK:])
        rows.append(cols[0] if len(cols) == 1 else jnp.concatenate(cols, axis=1))
    return rows[0] if len(rows) == 1 else jnp.concatenate(rows, axis=0)


def blk(i):
    if isinstance(i, int):
        return pl.ds(i * BLK, BLK)
    return pl.ds(pl.multiple_of(i * BLK, BLK), BLK)


def two(i, n=1):
    if isinstance(i, int):
        return pl.ds(i * PAIR, n * PAIR)
    return pl.ds(pl.multiple_of(i * PAIR, PAIR), n * PAIR)


def chunks(lo):
    first = lo // BLK
    for i in range(first, FRONT // BLK, CHUNK):
        yield i, min(CHUNK, FRONT // BLK - i)


def front_body(level, refs):
    last = level == LEVELS - 1
    ids = refs[0]
    if level == 0:
        pieces, refs = refs[1:11], refs[11:]
    else:
        mine, theirs, own_in, near_in, far_in = refs[1:6]
        refs = refs[8:]
    l_all, r_all, u_out = refs[:3]
    refs = refs[3:]
    if not last:
        give_out, refs = refs[0], refs[1:]
    F, G, C, UG, Ub, LL, Lf, T, D, E, WW, Lo, Ro, Uo, sem = refs
    rid = ids[8]
    core = ids[9]
    copies = []

    def take(src, r, half, lo, hi):
        i = 2 * r + half
        copies.append((src.at[:, pl.ds(0, 640)], G.at[i, pl.ds(lo, hi - lo), :]))
        at = pl.multiple_of(SEP + r * BLK + half * 64, 64)
        for side in range(2):
            if lo <= side * 64 < hi:
                copies.append(
                    (src.at[pl.ds(side * 64 - lo, 64), pl.ds(640, 512)], F.at[pl.ds(at, 64), pl.ds(side * 512, 512)])
                )
        if level == 0:
            copies.append((src.at[:, pl.ds(1152, 384)], UG.at[half, r, pl.ds(lo, hi - lo), :]))

    if level == 0:
        for n, half in ((0, core), (5, 1 - core)):
            take(pieces[n], rid, half, 0, BLK)
            take(pieces[n + 1], (rid + 3) % 4, half, 0, BLK)
            take(pieces[n + 2], (rid + 1) % 4, half, 0, BLK)
            take(pieces[n + 3], (rid + 2) % 4, half, 0, 64)
            take(pieces[n + 4], (rid + 2) % 4, half, 64, BLK)
    else:
        for src, half in ((mine, core), (theirs, 1 - core)):
            for r in range(4):
                take(src.at[r], r, half, 0, BLK)
        copies.append((own_in, UG.at[0]))
        copies.append((near_in, UG.at[1, core]))
        copies.append((far_in, UG.at[1, 1 - core]))
    copies = [pltpu.make_async_copy(s, t, sem.at[n]) for n, (s, t) in enumerate(copies)]
    for c in copies:
        c.start()
    C[...] = jnp.zeros_like(C)
    LL[...] = jnp.zeros_like(LL)
    T[...] = jnp.zeros_like(T)
    WW[...] = jnp.zeros_like(WW)
    for c in copies:
        c.wait()
    for i in range(NSEP):
        for d in range(5):
            j = (i - d) % NSEP
            part = G[i, :, BLK * d : BLK * d + BLK]
            if i >= j:
                F[blk(i), blk(j)] = part
            elif d < 4:
                F[blk(j), blk(i)] = part.T
    for child in range(2):
        parts = {}
        if level == 0:
            for r in range(NUPD):
                for d in range(3):
                    if d < 2 or r >= 2:
                        parts[r, (r - d) % NUPD] = UG[child, r, :, BLK * d : BLK * d + BLK]
        else:
            for half in range(2):
                for n, ij in enumerate(HALVES[half]):
                    parts[ij] = UG[child, half, :, BLK * n : BLK * n + BLK]
        for (i, j), part in parts.items():
            Ub[child, blk(i), blk(j)] = part
            if i != j:
                Ub[child, blk(j), blk(i)] = part.T

    def add_block(t, c):
        child = t // 10
        p = t % 10
        i = (p >= 1).astype(jnp.int32) + (p >= 3).astype(jnp.int32) + (p >= 6).astype(jnp.int32)
        j = p - i * (i + 1) // 2
        mi = ids[4 * child + i]
        mj = ids[4 * child + j]
        si = jnp.where(mi >= mj, i, j)
        sj = i + j - si
        hi = jnp.maximum(mi, mj)
        lo = jnp.minimum(mi, mj)

        @pl.when(lo < NSEP)
        def _():
            F[blk(hi), blk(lo)] += Ub[child, blk(si), blk(sj)]

        @pl.when(lo >= NSEP)
        def _():
            h = jnp.maximum(hi - NSEP, 0)
            l = jnp.maximum(lo - NSEP, 0)
            C[blk(h), blk(l)] += Ub[child, blk(si), blk(sj)]
            if last:

                @pl.when(i > j)
                def _():
                    C[blk(l), blk(h)] += Ub[child, blk(sj), blk(si)]

        return c

    lax.fori_loop(0, 20, add_block, 0)
    D[...] = F[:BLK, :BLK]

    def panel(k, lo):
        for i, n in chunks(lo):
            rows = pl.ds(i * BLK, n * BLK)
            v = nt4(stack_split(T[rows, :]), WW[...])
            Lf[rows, blk(k)] = v
            LL[two(i, n), blk(k)] = stack_split(v)

    def step(k, lo, depth):
        nxt = jnp.minimum(k + 1, NSEP - 1)
        panel(jnp.maximum(k - 1, 0), lo)
        for i, n in chunks(lo):
            rows = pl.ds(i * BLK, n * BLK)
            T[rows, :] = F[rows, blk(k)] - nt4(LL[two(i, n), :depth], LL[two(k), :depth])
        near = LL[two(nxt), :depth]
        E[...] = F[blk(nxt), blk(nxt)] - nt4(near, near)
        W = jnp.concatenate(block_inverse([D[8 * g : 8 * g + 8, :] for g in range(BLK // 8)]), axis=0)
        WW[...] = stack_split(W)
        l = stack_split(nt4(stack_split(T[blk(nxt), :]), WW[...]))
        D[...] = E[...] - nt4(l, l)

    lax.fori_loop(0, 4, lambda k, c: (step(k, 0, 384), c)[1], 0)
    lax.fori_loop(4, 8, lambda k, c: (step(k, 384, 896), c)[1], 0)
    panel(7, 896)
    rows = pl.ds(pl.multiple_of(rid * 256, 256), 256)
    ri = lax.broadcasted_iota(jnp.int32, (256, SEP), 0) + rid * 256
    ci = lax.broadcasted_iota(jnp.int32, (256, SEP), 1)
    Lo[...] = jnp.where(ri >= ci, Lf[rows, :], 0.0)
    Ro[...] = Lf[pl.ds(pl.multiple_of(SEP + rid * BLK, BLK), BLK), :]
    writes = [
        pltpu.make_async_copy(Lo, l_all.at[level], sem.at[0]),
        pltpu.make_async_copy(Ro, r_all.at[level], sem.at[1]),
    ]
    for c in writes:
        c.start()
    if last:
        mine_u = pl.ds(pl.multiple_of(rid * BLK, BLK), BLK)
        u_out[...] = C[mine_u, :] - nt4(LL[two(NSEP + rid), :], LL[two(NSEP, NUPD), :])
    else:
        place = {ij: (half, n) for half in range(2) for n, ij in enumerate(HALVES[half])}
        for i in range(NUPD):
            new = C[blk(i), : BLK * (i + 1)] - nt4(LL[two(NSEP + i), :], LL[two(NSEP, i + 1), :])
            for j in range(i + 1):
                half, n = place[i, j]
                Uo[half, :, BLK * n : BLK * n + BLK] = new[:, BLK * j : BLK * j + BLK]
        writes += [
            pltpu.make_async_copy(Uo, u_out, sem.at[2]),
            pltpu.make_async_copy(Uo.at[core], give_out, sem.at[3]),
        ]
        for c in writes[2:]:
            c.start()
    for c in writes:
        c.wait()


def front(level, ids, *inputs):
    smem = pl.BlockSpec(memory_space=pltpu.SMEM)
    vmem = pl.BlockSpec(memory_space=pltpu.VMEM)
    hbm = pl.BlockSpec(memory_space=pltpu.HBM)
    last = level == LEVELS - 1
    update = [(BLK, UPD)] if last else [(2, BLK, 640), (BLK, 640)]
    shapes = [(LEVELS, 256, SEP), (LEVELS, BLK, SEP)] + update
    return pl.pallas_call(
        lambda *refs: front_body(level, refs),
        in_specs=[smem] + [hbm] * len(inputs),
        out_specs=[hbm] * 2 + ([vmem] if last else [hbm] * 2),
        out_shape=[jax.ShapeDtypeStruct(s, f32) for s in shapes],
        input_output_aliases={} if level == 0 else {6: 0, 7: 1},
        scratch_shapes=[
            pltpu.VMEM((FRONT, SEP), f32),
            pltpu.VMEM((NSEP, BLK, 640), f32),
            pltpu.VMEM((UPD, UPD), f32),
            pltpu.VMEM((2, 4, BLK, 384) if level == 0 else (2, 2, BLK, 640), f32),
            pltpu.VMEM((2, UPD, UPD), f32),
            pltpu.VMEM((2 * FRONT, SEP), bf16),
            pltpu.VMEM((FRONT, SEP), f32),
            pltpu.VMEM((FRONT, BLK), f32),
            pltpu.VMEM((BLK, BLK), f32),
            pltpu.VMEM((BLK, BLK), f32),
            pltpu.VMEM((PAIR, BLK), bf16),
            pltpu.VMEM((256, SEP), f32),
            pltpu.VMEM((BLK, SEP), f32),
            pltpu.VMEM((2, BLK, 640), f32),
            pltpu.SemaphoreType.DMA((40,)),
        ],
        compiler_params=pltpu.CompilerParams(vmem_limit_bytes=60 << 20),
        cost_estimate=pl.CostEstimate(flops=20_000_000_000, transcendentals=0, bytes_accessed=20_000_000),
        name=f"front{level}",
    )(ids, *inputs)


def pack_body(with_child, refs):
    ids, sep, cpl = refs[:3]
    refs = refs[3:]
    if with_child:
        child, refs = refs[0], refs[1:]
    give, keep = refs[:2]
    rid = ids[0]
    core = ids[1]
    for out, half in ((give, 1 - core), (keep, core)):
        i = 2 * rid + half
        rows = pl.ds(pl.multiple_of(half * BLK, BLK), BLK)
        for d in range(5):
            out[:, BLK * d : BLK * d + BLK] = sep[0, rows, blk((i + NSEP - d) % NSEP)]
        for side in range(2):
            at = pl.ds(pl.multiple_of(half * 64, 64), 64)
            out[64 * side : 64 * side + 64, 640:] = cpl[0, at, 512 * side : 512 * side + 512]
    if with_child:
        for d in range(3):
            refs[2][:, BLK * d : BLK * d + BLK] = child[:, blk((rid + NUPD - d) % NUPD)]


def pack_shares(level, ids, sep, cpl, *child):
    return pl.pallas_call(
        lambda *refs: pack_body(len(child) > 0, refs),
        grid=(1,),
        in_specs=[
            pl.BlockSpec(memory_space=pltpu.SMEM),
            pl.BlockSpec((1, 256, SEP), lambda n: (level, 0, 0)),
            pl.BlockSpec((1, BLK, SEP), lambda n: (level, 0, 0)),
        ]
        + [pl.BlockSpec((BLK, UPD), lambda n: (0, 0))] * len(child),
        out_specs=[pl.BlockSpec((BLK, 1152), lambda n: (0, 0))] * 2
        + [pl.BlockSpec((BLK, 384), lambda n: (0, 0))] * len(child),
        out_shape=[jax.ShapeDtypeStruct((BLK, 1152), f32)] * 2
        + [jax.ShapeDtypeStruct((BLK, 384), f32)] * len(child),
        name=f"pack{level}",
    )(ids, sep, cpl, *child)


def swap(x, stride):
    return lax.ppermute(x, "leaf", [(i, i ^ 1 << stride) for i in range(lax.axis_size("leaf"))])


def shift(x, by):
    size = lax.axis_size("rows")
    return lax.ppermute(x, "rows", [(i, (i + by) % size) for i in range(size)])


def on_device(child_update, block_maps, sep_share, coupling_share):
    leaf = lax.axis_index("leaf")
    rid = lax.axis_index("rows")
    core = leaf & 1
    sep = sep_share[0]
    cpl = coupling_share[0]
    where = jnp.stack([rid, core]).astype(jnp.int32)

    tie = lax.optimization_barrier
    give, keep, child = pack_shares(0, where, sep, cpl, child_update[0])
    own = jnp.concatenate([keep + swap(give, 0), child], axis=1)
    own, after = tie((own, where))
    left = shift(own, 1)
    right = shift(own, -1)

    give, keep = pack_shares(1, after, sep, cpl)
    p1 = keep + swap(give, 0)
    got = swap(p1, 1)
    give, keep = pack_shares(2, after, sep, cpl)
    p2 = keep + swap(give, 0)
    p1, p2 = p1 + got, p2 + swap(p2, 1)
    p2 = p2 + swap(p2, 2)

    opp = [shift(left[:64], 1), shift(right[64:], -1)]
    far = [swap(x, 0) for x in (own, left, right)]
    opp, far, p1, p2 = tie((opp, far, p1, p2))
    near = [own, left, right] + opp
    far = far + [swap(x, 0) for x in opp]
    mine = [None] + [lax.all_gather(p, "rows", axis=0, tiled=False) for p in (p1, p2)]

    l_all = r_all = current = give = None
    for level in range(LEVELS):
        me = leaf >> level
        child_ids = (me - core, me - core + 1) if level == 0 else (me, me ^ 1)
        ids = jnp.concatenate(
            [lax.dynamic_index_in_dim(block_maps[level], i, 0, keepdims=False) for i in child_ids] + [where]
        )
        if level == 0:
            l_all, r_all, current, give = front(0, ids, *near, *far)
            mine[1], give = tie((mine[1], give))
            continue
        got = swap(give, level)
        inputs = (mine[level], swap(mine[level], 0), current, got, swap(got, 0), l_all, r_all)
        if level == 1:
            l_all, r_all, current, give = front(1, ids, *inputs)
            mine[2], give = tie((mine[2], give))
        else:
            l_all, r_all, top = front(2, ids, *inputs)
    return l_all[None], r_all[None], top[None]


def solution(mesh):
    return jax.shard_map(
        on_device,
        mesh=mesh,
        in_specs=(
            P("leaf", "rows", None),
            P(),
            P("leaf", None, "rows", None),
            P("leaf", None, "rows", None),
        ),
        out_specs=(
            P("leaf", None, "rows", None),
            P("leaf", None, "rows", None),
            P("leaf", "rows", None),
        ),
        check_vma=False,
    )
```

profile of v0, /device:TPU:1, one launch (start us, length us, event | category | flops | bytes accessed | tf_op | source)
XLA Modules:
  0.0 222.2 jit_solution(17190755857618856391)
XLA Ops:
  7.9 2.6 %pack0.1 = (f32[128,1152]{1,0:T(8,128)}, f32[128,1152]{1,0:T(8,128)}, f32[128,384]{1,0:T(8,128)}) custom-call(s32[2]{0:T(128)} %pad_add_fusion.refs_0_, f32[3,256,1024]{2,1,0:T(8,128)} %bitcast.10, f32[3,128,1024]{2,1,0:T(8,128)} %bitcast.13, f32[128,512]{1,0:T(8,128)} %bitcast.16), custom_call_target="tpu_custom_call" | custom-call | tf_op jit(solution)/shard_map/pack0/pallas_call | solution.py:364
  10.5 1.4 collective-permute-start
  11.9 1.8 collective-permute-done
  15.9 2.8 %pack2.1 = (f32[128,1152]{1,0:T(8,128)}, f32[128,1152]{1,0:T(8,128)}) custom-call(s32[2]{0:T(128)} %pad_add_fusion.refs_0_, f32[3,256,1024]{2,1,0:T(8,128)} %bitcast.11, f32[3,128,1024]{2,1,0:T(8,128)} %bitcast.14), custom_call_target="tpu_custom_call" | custom-call | tf_op jit(solution)/shard_map/pack2/pallas_call | solution.py:364
  19.1 2.5 %pack1.1 = (f32[128,1152]{1,0:T(8,128)}, f32[128,1152]{1,0:T(8,128)}) custom-call(s32[2]{0:T(128)} %pad_add_fusion.refs_0_, f32[3,256,1024]{2,1,0:T(8,128)} %bitcast.12, f32[3,128,1024]{2,1,0:T(8,128)} %bitcast.15), custom_call_target="tpu_custom_call" | custom-call | tf_op jit(solution)/shard_map/pack1/pallas_call | solution.py:364
  21.8 1.5 collective-permute-start.11
  23.3 1.2 collective-permute-start.1
  24.5 1.5 collective-permute-start.3
  27.3 9.3 %collective-permute-done.11 = f32[128,1152]{1,0:T(8,128)S(1)} collective-permute-done((f32[128,1152]{1,0:T(8,128)S(1)}, f32[128,1152]{1,0:T(8,128)S(1)}, u32[]{:S(2)}, u32[]{:S(2)}) %collective-permute-start.11) | collective-permute-done | bytes 589856 | tf_op jit(solution)/shard_map/ppermute | solution.py:382
  36.7 3.1 %collective-permute-start.12 = (f32[128,1152]{1,0:T(8,128)S(1)}, f32[128,1152]{1,0:T(8,128)S(1)}, u32[]{:S(2)}, u32[]{:S(2)}) collective-permute-start(f32[128,1152]{1,0:T(8,128)S(1)} %add.48), channel_id=1, source_target_pairs={{0,16},{4,20},{8,24},{12,28},{16,0},{20,4},{24,8},{28,12},{32,48},... | collective-permute-start | bytes 1769480 | tf_op jit(solution)/shard_map/ppermute | solution.py:382
  39.7 2.1 collective-permute-start.5
  41.8 1.1 collective-permute-done.1.refs_2_
  43.0 1.5 collective-permute-start.6
  45.6 3.5 %collective-permute-done.9 = f32[128,1152]{1,0:T(8,128)S(1)} collective-permute-done((f32[128,1152]{1,0:T(8,128)S(1)}, f32[128,1152]{1,0:T(8,128)S(1)}, u32[]{:S(2)}, u32[]{:S(2)}) %collective-permute-start.9) | collective-permute-done | bytes 589856 | tf_op jit(solution)/shard_map/ppermute | solution.py:382
  49.1 1.3 collective-permute-start.2
  50.4 13.9 %collective-permute-done.12 = f32[128,1152]{1,0:T(8,128)S(1)} collective-permute-done((f32[128,1152]{1,0:T(8,128)S(1)}, f32[128,1152]{1,0:T(8,128)S(1)}, u32[]{:S(2)}, u32[]{:S(2)}) %collective-permute-start.12) | collective-permute-done | bytes 589856 | tf_op jit(solution)/shard_map/ppermute | solution.py:382
  64.3 2.5 %collective-permute-start.4 = (f32[64,1536]{1,0:T(8,128)S(1)}, f32[64,1536]{1,0:T(8,128)}, u32[]{:S(2)}, u32[]{:S(2)}) collective-permute-start(f32[64,1536]{1,0:T(8,128)S(1)} %slice.24), channel_id=1, source_target_pairs={{0,3},{1,0},{2,1},{3,2},{4,7},{5,4},{6,5},{7,6},{8,11},{9,8},{10,9... | collective-permute-start | bytes 1179656 | tf_op jit(solution)/shard_map/ppermute | solution.py:387
  68.7 5.3 %collective-permute-done.4.refs_5_ = f32[64,1536]{1,0:T(8,128)} collective-permute-done((f32[64,1536]{1,0:T(8,128)S(1)}, f32[64,1536]{1,0:T(8,128)}, u32[]{:S(2)}, u32[]{:S(2)}) %collective-permute-start.4) | collective-permute-done | bytes 393248 | tf_op jit(solution)/shard_map/ppermute | solution.py:387
  74.1 2.2 collective-permute-start.13
  79.4 35.8 %front0.1 = (f32[3,256,1024]{2,1,0:T(8,128)}, f32[3,128,1024]{2,1,0:T(8,128)}, f32[2,128,640]{2,1,0:T(8,128)}, f32[128,640]{1,0:T(8,128)}) custom-call(s32[10]{0:T(128)} %add_add_fusion.2.refs_0_, f32[128,1536]{1,0:T(8,128)} %copy-done, f32[128,1536]{1,0:T(8,128)} %copy-done.2, f32[128,1536]{1,0:T(8,128)} %collective-permute-done.3.refs_3_, ...), custom_call_target="tpu_custom_call" | custom-call | flops 20000000000 | bytes 20000000 | tf_op jit(solution)/shard_map/front0/pallas_call | solution.py:313
  115.8 9.4 %collective-permute-done.16.refs_4_ = f32[128,640]{1,0:T(8,128)S(1)} collective-permute-done((f32[128,640]{1,0:T(8,128)}, f32[128,640]{1,0:T(8,128)S(1)}, u32[]{:S(2)}, u32[]{:S(2)}) %collective-permute-start.16) | collective-permute-done | bytes 327712 | tf_op jit(solution)/shard_map/ppermute | solution.py:382
  129.0 35.8 %front1.1 = (f32[3,256,1024]{2,1,0:T(8,128)}, f32[3,128,1024]{2,1,0:T(8,128)}, f32[2,128,640]{2,1,0:T(8,128)}, f32[128,640]{1,0:T(8,128)}) custom-call(s32[10]{0:T(128)} %add_add_fusion.1.refs_0_, f32[4,128,1152]{2,1,0:T(8,128)} %bitcast.18, f32[4,128,1152]{2,1,0:T(8,128)} %copy-done.5, ...), custom_call_target="tpu_custom_call", output_to_operand_aliasing={{0}: (6, {}), {1}: (7, {})} | custom-call | flops 20000000000 | bytes 20000000 | tf_op jit(solution)/shard_map/front1/pallas_call | solution.py:313
  165.6 10.5 %collective-permute-done.19.refs_4_ = f32[128,640]{1,0:T(8,128)S(1)} collective-permute-done((f32[128,640]{1,0:T(8,128)}, f32[128,640]{1,0:T(8,128)S(1)}, u32[]{:S(2)}, u32[]{:S(2)}) %collective-permute-start.19) | collective-permute-done | bytes 327712 | tf_op jit(solution)/shard_map/ppermute | solution.py:382
  179.9 35.5 %front2.1 = (f32[3,256,1024]{2,1,0:T(8,128)}, f32[3,128,1024]{2,1,0:T(8,128)}, f32[128,512]{1,0:T(8,128)}) custom-call(s32[10]{0:T(128)} %add_add_fusion.refs_0_, f32[4,128,1152]{2,1,0:T(8,128)} %bitcast.20, f32[4,128,1152]{2,1,0:T(8,128)} %copy-done.4, f32[2,128,640]{2,1,0:T(8,128)} %get-tuple-element.58.refs_3_, ...), custom_call_target="tpu_custom_call", output_to_operand_aliasing={{0}: (6, {}), {1}: (7, {})} | custom-call | flops 20000000000 | bytes 20000000 | tf_op jit(solution)/shard_map/front2/pallas_call | solution.py:313
  (70 shorter events, 20.0 us)
Async XLA Ops:
  7.2 108.1 %all-gather.7.cloned.1.call-start = ((), (), s32[]{:S(2)}) async-start(), calls=%async_computation.1 | async-start | bytes 2949120 | tf_op jit(solution)/shard_map/all_gather | solution.py:418
  10.5 3.3 %collective-permute-start = (f32[128,1152]{1,0:T(8,128)}, f32[128,1152]{1,0:T(8,128)S(1)}, u32[]{:S(2)}, u32[]{:S(2)}) collective-permute-start(f32[128,1152]{1,0:T(8,128)} %get-tuple-element.35), channel_id=1, source_target_pairs={{0,4},{4,0},{8,12},{12,8},{16,20},{20,16},{24,28},{28,24},{32,36},... | collective-permute-start | bytes 1769480 | tf_op jit(solution)/shard_map/ppermute | solution.py:382
  18.7 3.1 %collective-permute-start.10 = (f32[128,1152]{1,0:T(8,128)}, f32[128,1152]{1,0:T(8,128)S(1)}, u32[]{:S(2)}, u32[]{:S(2)}) collective-permute-start(f32[128,1152]{1,0:T(8,128)} %get-tuple-element.42), channel_id=1, source_target_pairs={{0,4},{4,0},{8,12},{12,8},{16,20},{20,16},{24,28},{28,24},{32,36},... | collective-permute-start | bytes 1769480 | tf_op jit(solution)/shard_map/ppermute | solution.py:382
  21.6 4.4 %collective-permute-start.8 = (f32[128,1152]{1,0:T(8,128)}, f32[128,1152]{1,0:T(8,128)S(1)}, u32[]{:S(2)}, u32[]{:S(2)}) collective-permute-start(f32[128,1152]{1,0:T(8,128)} %get-tuple-element.40), channel_id=1, source_target_pairs={{0,4},{4,0},{8,12},{12,8},{16,20},{20,16},{24,28},{28,24},{32,36},... | collective-permute-start | bytes 1769480 | tf_op jit(solution)/shard_map/ppermute | solution.py:382
  21.8 14.8 %collective-permute-start.11 = (f32[128,1152]{1,0:T(8,128)S(1)}, f32[128,1152]{1,0:T(8,128)S(1)}, u32[]{:S(2)}, u32[]{:S(2)}) collective-permute-start(f32[128,1152]{1,0:T(8,128)S(1)} %add.47), channel_id=1, source_target_pairs={{0,8},{4,12},{8,0},{12,4},{16,24},{20,28},{24,16},{28,20},{32,40},... | collective-permute-start | bytes 1769480 | tf_op jit(solution)/shard_map/ppermute | solution.py:382
  23.3 19.7 %collective-permute-start.1 = (f32[128,1536]{1,0:T(8,128)S(1)}, f32[128,1536]{1,0:T(8,128)S(1)}, u32[]{:S(2)}, u32[]{:S(2)}) collective-permute-start(f32[128,1536]{1,0:T(8,128)S(1)} %pad_maximum_fusion.refs_1_), channel_id=1, source_target_pairs={{0,1},{1,2},{2,3},{3,0},{4,5},{5,6},{6,7},{7,4},{8,9},{9,10},{10,1... | collective-permute-start | bytes 2359304 | tf_op jit(solution)/shard_map/ppermute | solution.py:387
  24.5 20.0 %collective-permute-start.3 = (f32[128,1536]{1,0:T(8,128)S(1)}, f32[128,1536]{1,0:T(8,128)}, u32[]{:S(2)}, u32[]{:S(2)}) collective-permute-start(f32[128,1536]{1,0:T(8,128)S(1)} %pad_maximum_fusion.refs_1_), channel_id=1, source_target_pairs={{0,3},{1,0},{2,1},{3,2},{4,7},{5,4},{6,5},{7,6},{8,11},{9,8},{10,9... | collective-permute-start | bytes 2359304 | tf_op jit(solution)/shard_map/ppermute | solution.py:387
  27.1 22.0 %collective-permute-start.9 = (f32[128,1152]{1,0:T(8,128)S(1)}, f32[128,1152]{1,0:T(8,128)S(1)}, u32[]{:S(2)}, u32[]{:S(2)}) collective-permute-start(f32[128,1152]{1,0:T(8,128)S(1)} %add.45), channel_id=1, source_target_pairs={{0,8},{4,12},{8,0},{12,4},{16,24},{20,28},{24,16},{28,20},{32,40},... | collective-permute-start | bytes 1769480 | tf_op jit(solution)/shard_map/ppermute | solution.py:382
  36.7 27.6 %collective-permute-start.12 = (f32[128,1152]{1,0:T(8,128)S(1)}, f32[128,1152]{1,0:T(8,128)S(1)}, u32[]{:S(2)}, u32[]{:S(2)}) collective-permute-start(f32[128,1152]{1,0:T(8,128)S(1)} %add.48), channel_id=1, source_target_pairs={{0,16},{4,20},{8,24},{12,28},{16,0},{20,4},{24,8},{28,12},{32,48},... | collective-permute-start | bytes 1769480 | tf_op jit(solution)/shard_map/ppermute | solution.py:382
  39.7 29.0 %collective-permute-start.5 = (f32[128,1536]{1,0:T(8,128)S(1)}, f32[128,1536]{1,0:T(8,128)}, u32[]{:S(2)}, u32[]{:S(2)}) collective-permute-start(f32[128,1536]{1,0:T(8,128)S(1)} %pad_maximum_fusion.refs_1_), channel_id=1, source_target_pairs={{0,4},{4,0},{8,12},{12,8},{16,20},{20,16},{24,28},{28,24},{32,36},... | collective-permute-start | bytes 2359304 | tf_op jit(solution)/shard_map/ppermute | solution.py:382
  43.0 31.1 %collective-permute-start.6 = (f32[128,1536]{1,0:T(8,128)S(1)}, f32[128,1536]{1,0:T(8,128)}, u32[]{:S(2)}, u32[]{:S(2)}) collective-permute-start(f32[128,1536]{1,0:T(8,128)S(1)} %collective-permute-done.1.refs_2_), channel_id=1, source_target_pairs={{0,4},{4,0},{8,12},{12,8},{16,20},{20,16},{24,28},{28,24},{32,36},... | collective-permute-start | bytes 2359304 | tf_op jit(solution)/shard_map/ppermute | solution.py:382
  44.5 29.6 %collective-permute-start.7 = (f32[128,1536]{1,0:T(8,128)}, f32[128,1536]{1,0:T(8,128)}, u32[]{:S(2)}, u32[]{:S(2)}) collective-permute-start(f32[128,1536]{1,0:T(8,128)} %collective-permute-done.3.refs_3_), channel_id=1, source_target_pairs={{0,4},{4,0},{8,12},{12,8},{16,20},{20,16},{24,28},{28,24},{32,36},... | collective-permute-start | bytes 2359304 | tf_op jit(solution)/shard_map/ppermute | solution.py:382
  44.6 32.0 %copy-start.3 = (s32[3,32,4]{1,2,0:T(4,128)S(1)}, s32[3,32,4]{1,2,0:T(4,128)}, u32[]{:S(2)}) copy-start(s32[3,32,4]{1,2,0:T(4,128)} %param.5) | copy-start | bytes 4612
  49.1 19.6 %collective-permute-start.2 = (f32[64,1536]{1,0:T(8,128)S(1)}, f32[64,1536]{1,0:T(8,128)}, u32[]{:S(2)}, u32[]{:S(2)}) collective-permute-start(f32[64,1536]{1,0:T(8,128)S(1)} %slice.23), channel_id=1, source_target_pairs={{0,1},{1,2},{2,3},{3,0},{4,5},{5,6},{6,7},{7,4},{8,9},{9,10},{10,1... | collective-permute-start | bytes 1179656 | tf_op jit(solution)/shard_map/ppermute | solution.py:387
  64.3 9.7 %collective-permute-start.4 = (f32[64,1536]{1,0:T(8,128)S(1)}, f32[64,1536]{1,0:T(8,128)}, u32[]{:S(2)}, u32[]{:S(2)}) collective-permute-start(f32[64,1536]{1,0:T(8,128)S(1)} %slice.24), channel_id=1, source_target_pairs={{0,3},{1,0},{2,1},{3,2},{4,7},{5,4},{6,5},{7,6},{8,11},{9,8},{10,9... | collective-permute-start | bytes 1179656 | tf_op jit(solution)/shard_map/ppermute | solution.py:387
  74.1 90.7 %all-gather.5.cloned.1.call-start = ((), (), s32[]{:S(2)}) async-start(), calls=%async_computation | async-start | bytes 2949120 | tf_op jit(solution)/shard_map/all_gather | solution.py:418
  74.1 3.7 %collective-permute-start.13 = (f32[64,1536]{1,0:T(8,128)}, f32[64,1536]{1,0:T(8,128)S(1)}, u32[]{:S(2)}, u32[]{:S(2)}) collective-permute-start(f32[64,1536]{1,0:T(8,128)} %collective-permute-done.2.refs_4_), channel_id=1, source_target_pairs={{0,4},{4,0},{8,12},{12,8},{16,20},{20,16},{24,28},{28,24},{32,36},... | collective-permute-start | bytes 1179656 | tf_op jit(solution)/shard_map/ppermute | solution.py:382
  76.3 2.1 collective-permute-start.14
  115.3 12.2 %collective-permute-start.15 = (f32[4,128,1152]{2,1,0:T(8,128)}, f32[4,128,1152]{2,1,0:T(8,128)S(1)}, u32[]{:S(2)}, u32[]{:S(2)}) collective-permute-start(f32[4,128,1152]{2,1,0:T(8,128)} %bitcast.17), channel_id=1, source_target_pairs={{0,4},{4,0},{8,12},{12,8},{16,20},{20,16},{24,28},{28,24},{32,36},... | collective-permute-start | bytes 7077896 | tf_op jit(solution)/shard_map/ppermute | solution.py:382
  115.8 9.5 %collective-permute-start.16 = (f32[128,640]{1,0:T(8,128)}, f32[128,640]{1,0:T(8,128)S(1)}, u32[]{:S(2)}, u32[]{:S(2)}) collective-permute-start(f32[128,640]{1,0:T(8,128)} %get-tuple-element.53), channel_id=1, source_target_pairs={{0,8},{4,12},{8,0},{12,4},{16,24},{20,28},{24,16},{28,20},{32,40},... | collective-permute-start | bytes 983048 | tf_op jit(solution)/shard_map/ppermute | solution.py:382
  125.2 2.2 collective-permute-start.17
  164.8 13.6 %collective-permute-start.18 = (f32[4,128,1152]{2,1,0:T(8,128)}, f32[4,128,1152]{2,1,0:T(8,128)S(1)}, u32[]{:S(2)}, u32[]{:S(2)}) collective-permute-start(f32[4,128,1152]{2,1,0:T(8,128)} %bitcast.19), channel_id=1, source_target_pairs={{0,4},{4,0},{8,12},{12,8},{16,20},{20,16},{24,28},{28,24},{32,36},... | collective-permute-start | bytes 7077896 | tf_op jit(solution)/shard_map/ppermute | solution.py:382
  165.3 10.9 %collective-permute-start.19 = (f32[128,640]{1,0:T(8,128)}, f32[128,640]{1,0:T(8,128)S(1)}, u32[]{:S(2)}, u32[]{:S(2)}) collective-permute-start(f32[128,640]{1,0:T(8,128)} %get-tuple-element.59), channel_id=1, source_target_pairs={{0,16},{4,20},{8,24},{12,28},{16,0},{20,4},{24,8},{28,12},{32,48},... | collective-permute-start | bytes 983048 | tf_op jit(solution)/shard_map/ppermute | solution.py:382
  176.1 2.2 collective-permute-start.20
  (11 other events, 63.2 us)
Sparse Core Ops, SparseCore 0:
  74.2 34.9 all-gather.6
  115.9 33.0 all-gather.4
where the time goes:
time: 223 us; the launch traced here: 222 us
  Pallas kernels  115 us (52%)
  waiting for transfers between devices  57.1 us (26%)
  starting transfers between devices  22.6 us (10%)
  between operations  14.2 us (6%)
  other arithmetic  7.71 us (3%)
  local copies, waits for them, and re-layouts  5.55 us (2%)
    pallas_call x3, Pallas kernels, front(): pl.pallas_call(lambda *refs: front_body(level, refs), in_specs=[smem] + [...  107 us
    ppermute x17, waiting for transfers between devices, swap(): lax.ppermute(x, 'leaf', [(i, i ^ 1 << stride) for i in range(lax.axis_siz...  50.6 us
    ppermute x17, starting transfers between devices, swap(): lax.ppermute(x, 'leaf', [(i, i ^ 1 << stride) for i in range(lax.axis_siz...  16.1 us
    pallas_call x3, Pallas kernels, pack_shares(): pl.pallas_call(lambda *refs: pack_body(len(child) > 0, refs), grid=(1,),...  7.93 us
    ppermute x4, waiting for transfers between devices, shift(): return lax.ppermute(x, 'rows', [(i, (i + by) % size) for i in range(size)])  6.45 us
    ppermute x4, starting transfers between devices, shift(): return lax.ppermute(x, 'rows', [(i, (i + by) % size) for i in range(size)])  6.45 us
  transfers between devices with their start and end apart: 23, of which 12 were waited for; matrix products, arithmetic and copies ran while one was open for 3% of the time, Pallas kernels for 33%

commit v1 on v0

--- a/solution.py
+++ b/solution.py
@@ -339,43 +339,32 @@
     )(ids, *inputs)
 
 
-def pack_body(with_child, refs):
-    ids, sep, cpl = refs[:3]
-    refs = refs[3:]
-    if with_child:
-        child, refs = refs[0], refs[1:]
-    give, keep = refs[:2]
+def pack_body(ids, sep, cpl, child, *outs):
     rid = ids[0]
     core = ids[1]
-    for out, half in ((give, 1 - core), (keep, core)):
-        i = 2 * rid + half
-        rows = pl.ds(pl.multiple_of(half * BLK, BLK), BLK)
-        for d in range(5):
-            out[:, BLK * d : BLK * d + BLK] = sep[0, rows, blk((i + NSEP - d) % NSEP)]
-        for side in range(2):
-            at = pl.ds(pl.multiple_of(half * 64, 64), 64)
-            out[64 * side : 64 * side + 64, 640:] = cpl[0, at, 512 * side : 512 * side + 512]
-    if with_child:
-        for d in range(3):
-            refs[2][:, BLK * d : BLK * d + BLK] = child[:, blk((rid + NUPD - d) % NUPD)]
-
-
-def pack_shares(level, ids, sep, cpl, *child):
+    for d in range(3):
+        outs[0][:, BLK * d : BLK * d + BLK] = child[:, blk((rid + NUPD - d) % NUPD)]
+    for level in range(LEVELS):
+        for out, half in ((outs[1 + 2 * level], 1 - core), (outs[2 + 2 * level], core)):
+            i = 2 * rid + half
+            rows = pl.ds(pl.multiple_of(half * BLK, BLK), BLK)
+            for d in range(5):
+                out[:, BLK * d : BLK * d + BLK] = sep[level, rows, blk((i + NSEP - d) % NSEP)]
+            for side in range(2):
+                at = pl.ds(pl.multiple_of(half * 64, 64), 64)
+                out[64 * side : 64 * side + 64, 640:] = cpl[level, at, 512 * side : 512 * side + 512]
+
+
+def pack_shares(ids, sep, cpl, child):
+    vmem = pl.BlockSpec(memory_space=pltpu.VMEM)
     return pl.pallas_call(
-        lambda *refs: pack_body(len(child) > 0, refs),
-        grid=(1,),
-        in_specs=[
-            pl.BlockSpec(memory_space=pltpu.SMEM),
-            pl.BlockSpec((1, 256, SEP), lambda n: (level, 0, 0)),
-            pl.BlockSpec((1, BLK, SEP), lambda n: (level, 0, 0)),
-        ]
-        + [pl.BlockSpec((BLK, UPD), lambda n: (0, 0))] * len(child),
-        out_specs=[pl.BlockSpec((BLK, 1152), lambda n: (0, 0))] * 2
-        + [pl.BlockSpec((BLK, 384), lambda n: (0, 0))] * len(child),
-        out_shape=[jax.ShapeDtypeStruct((BLK, 1152), f32)] * 2
-        + [jax.ShapeDtypeStruct((BLK, 384), f32)] * len(child),
-        name=f"pack{level}",
-    )(ids, sep, cpl, *child)
+        pack_body,
+        in_specs=[pl.BlockSpec(memory_space=pltpu.SMEM)] + [vmem] * 3,
+        out_specs=[vmem] * 7,
+        out_shape=[jax.ShapeDtypeStruct((BLK, 384), f32)] + [jax.ShapeDtypeStruct((BLK, 1152), f32)] * 6,
+        compiler_params=pltpu.CompilerParams(vmem_limit_bytes=24 << 20),
+        name="pack",
+    )(ids, sep, cpl, child)
 
 
 def swap(x, stride):
@@ -385,6 +374,10 @@
 def shift(x, by):
     size = lax.axis_size("rows")
     return lax.ppermute(x, "rows", [(i, (i + by) % size) for i in range(size)])
+
+
+def turn(x, by):
+    return lax.ppermute(x, "leaf", [(i, i ^ (by << 1)) for i in range(lax.axis_size("leaf"))])
 
 
 def on_device(child_update, block_maps, sep_share, coupling_share):
@@ -396,26 +389,21 @@
     where = jnp.stack([rid, core]).astype(jnp.int32)
 
     tie = lax.optimization_barrier
-    give, keep, child = pack_shares(0, where, sep, cpl, child_update[0])
-    own = jnp.concatenate([keep + swap(give, 0), child], axis=1)
-    own, after = tie((own, where))
+    tie = lax.optimization_barrier
+    child, give0, keep0, give1, keep1, give2, keep2 = pack_shares(where, sep, cpl, child_update[0])
+    own = jnp.concatenate([keep0 + swap(give0, 0), child], axis=1)
     left = shift(own, 1)
     right = shift(own, -1)
-
-    give, keep = pack_shares(1, after, sep, cpl)
-    p1 = keep + swap(give, 0)
-    got = swap(p1, 1)
-    give, keep = pack_shares(2, after, sep, cpl)
-    p2 = keep + swap(give, 0)
-    p1, p2 = p1 + got, p2 + swap(p2, 1)
-    p2 = p2 + swap(p2, 2)
-
+    p1 = keep1 + swap(give1, 0)
+    p1 = p1 + swap(p1, 1)
+    p2 = keep2 + swap(give2, 0)
     opp = [shift(left[:64], 1), shift(right[64:], -1)]
     far = [swap(x, 0) for x in (own, left, right)]
     opp, far, p1, p2 = tie((opp, far, p1, p2))
     near = [own, left, right] + opp
     far = far + [swap(x, 0) for x in opp]
-    mine = [None] + [lax.all_gather(p, "rows", axis=0, tiled=False) for p in (p1, p2)]
+    mine = [None, lax.all_gather(p1, "rows", axis=0, tiled=False), None]
+    others = [turn(p2, by) for by in (1, 2, 3)]
 
     l_all = r_all = current = give = None
     for level in range(LEVELS):
@@ -426,7 +414,8 @@
         )
         if level == 0:
             l_all, r_all, current, give = front(0, ids, *near, *far)
-            mine[1], give = tie((mine[1], give))
+            p2, mine[1], current, give = tie((p2, mine[1], current, give))
+            mine[2] = lax.all_gather(p2 + others[0] + others[1] + others[2], "rows", axis=0, tiled=False)
             continue
         got = swap(give, level)
         inputs = (mine[level], swap(mine[level], 0), current, got, swap(got, 0), l_all, r_all)

time: 223 us -> 201 us (0.901)
  waiting for transfers between devices: 57.1 us -> 43 us
  Pallas kernels: 115 us -> 108 us
  other arithmetic: 7.71 us -> 4.28 us
  local copies, waits for them, and re-layouts: 5.55 us -> 8.71 us
    ppermute x17 -> x15, waiting for transfers between devices: 50.6 us -> 20.3 us  [swap(): lax.ppermute(x, 'leaf', [(i, i ^ 1 << stride) for i in range(lax.axis_siz...]
    ppermute x4, waiting for transfers between devices: 6.45 us -> 22.6 us  [shift(): return lax.ppermute(x, 'rows', [(i, (i + by) % size) for i in range(size)])]
    pallas_call x3 -> x1, Pallas kernels: 7.93 us -> 0.92 us  [pack_shares(): pl.pallas_call(pack_body, in_specs=[pl.BlockSpec(memory_space=pltpu.SMEM)...]
    ppermute x0 -> x3, starting transfers between devices: none -> 3.92 us  [turn(): lax.ppermute(x, 'leaf', [(i, i ^ by << 1) for i in range(lax.axis_size('l...]
    unnamed x24 -> x28, local copies, waits for them, and re-layouts: 4.06 us -> 7.23 us
    ppermute x17 -> x15, starting transfers between devices: 16.1 us -> 13 us  [swap(): lax.ppermute(x, 'leaf', [(i, i ^ 1 << stride) for i in range(lax.axis_siz...]
  transfers between devices with their start and end apart: 23 -> 24, of which waited for: 12 -> 8; matrix products, arithmetic and copies ran while one was open for 3% -> 3% of each run, Pallas kernels for 33% -> 36%
where the time goes in v1:
time: 201 us
  Pallas kernels  108 us (54%)
  waiting for transfers between devices  43 us (21%)
  starting transfers between devices  22.5 us (11%)
  between operations  14.2 us (7%)
  local copies, waits for them, and re-layouts  8.71 us (4%)
  other arithmetic  4.28 us (2%)
    pallas_call x3, Pallas kernels, front(): pl.pallas_call(lambda *refs: front_body(level, refs), in_specs=[smem] + [...  107 us
    ppermute x4, waiting for transfers between devices, shift(): return lax.ppermute(x, 'rows', [(i, (i + by) % size) for i in range(size)])  22.6 us
    ppermute x15, waiting for transfers between devices, swap(): lax.ppermute(x, 'leaf', [(i, i ^ 1 << stride) for i in range(lax.axis_siz...  20.3 us
    ppermute x15, starting transfers between devices, swap(): lax.ppermute(x, 'leaf', [(i, i ^ 1 << stride) for i in range(lax.axis_siz...  13 us
    unnamed x28, local copies, waits for them, and re-layouts  7.23 us
    ppermute x4, starting transfers between devices, shift(): return lax.ppermute(x, 'rows', [(i, (i + by) % size) for i in range(size)])  5.5 us
  transfers between devices with their start and end apart: 24, of which 8 were waited for; matrix products, arithmetic and copies ran while one was open for 3% of the time, Pallas kernels for 36%

profile of v1, /device:TPU:1, one launch (start us, length us, event | category | flops | bytes accessed | tf_op | source)
XLA Modules:
  0.0 200.8 jit_solution(6302634861278724989)
XLA Ops:
  7.3 1.9 copy-done
  9.2 1.4 copy-done.1
  12.5 1.5 collective-permute-start
  14.1 1.5 collective-permute-done
  15.8 1.4 collective-permute-start.1
  17.1 1.4 collective-permute-start.3
  19.5 1.5 collective-permute-start.9
  21.2 14.5 %collective-permute-done.1.refs_2_ = f32[128,1536]{1,0:T(8,128)S(1)} collective-permute-done((f32[128,1536]{1,0:T(8,128)S(1)}, f32[128,1536]{1,0:T(8,128)S(1)}, u32[]{:S(2)}, u32[]{:S(2)}) %collective-permute-start.1) | collective-permute-done | bytes 786464 | tf_op jit(solution)/shard_map/ppermute | solution.py:376
  35.8 1.2 collective-permute-start.6
  37.2 1.0 slice.24
  38.3 1.3 collective-permute-start.2
  39.5 1.5 collective-permute-start.4
  42.0 7.9 %collective-permute-done.2.refs_4_ = f32[64,1536]{1,0:T(8,128)S(1)} collective-permute-done((f32[64,1536]{1,0:T(8,128)S(1)}, f32[64,1536]{1,0:T(8,128)S(1)}, u32[]{:S(2)}, u32[]{:S(2)}) %collective-permute-start.2) | collective-permute-done | bytes 393248 | tf_op jit(solution)/shard_map/ppermute | solution.py:376
  50.2 1.2 collective-permute-start.11
  52.3 1.3 collective-permute-start.13
  53.6 2.6 %collective-permute-start.14 = (f32[128,1152]{1,0:T(8,128)S(1)}, f32[128,1152]{1,0:T(8,128)S(1)}, u32[]{:S(2)}, u32[]{:S(2)}) collective-permute-start(f32[128,1152]{1,0:T(8,128)S(1)} %add.50), channel_id=1, source_target_pairs={{0,16},{4,20},{8,24},{12,28},{16,0},{20,4},{24,8},{28,12},{32,48},... | collective-permute-start | bytes 1769480 | tf_op jit(solution)/shard_map/ppermute | solution.py:380
  57.0 35.9 %front0.1 = (f32[3,256,1024]{2,1,0:T(8,128)}, f32[3,128,1024]{2,1,0:T(8,128)}, f32[2,128,640]{2,1,0:T(8,128)}, f32[128,640]{1,0:T(8,128)}) custom-call(s32[10]{0:T(128)} %add_add_fusion.2.refs_0_, f32[128,1536]{1,0:T(8,128)} %copy-done.3, f32[128,1536]{1,0:T(8,128)} %copy-done.4, f32[128,1536]{1,0:T(8,128)} %collective-permute-done.3.refs_3_, ...), custom_call_target="tpu_custom_call" | custom-call | flops 20000000000 | bytes 20000000 | tf_op jit(solution)/shard_map/front0/pallas_call | solution.py:313
  92.9 1.3 collective-permute-start.16
  94.2 1.1 add_add_fusion
  95.4 9.2 %collective-permute-done.17.refs_4_ = f32[128,640]{1,0:T(8,128)S(1)} collective-permute-done((f32[128,640]{1,0:T(8,128)S(1)}, f32[128,640]{1,0:T(8,128)S(1)}, u32[]{:S(2)}, u32[]{:S(2)}) %collective-permute-start.17) | collective-permute-done | bytes 327712 | tf_op jit(solution)/shard_map/ppermute | solution.py:371
  107.5 35.8 %front1.1 = (f32[3,256,1024]{2,1,0:T(8,128)}, f32[3,128,1024]{2,1,0:T(8,128)}, f32[2,128,640]{2,1,0:T(8,128)}, f32[128,640]{1,0:T(8,128)}) custom-call(s32[10]{0:T(128)} %add_add_fusion.3.refs_0_, f32[4,128,1152]{2,1,0:T(8,128)} %bitcast.14, f32[4,128,1152]{2,1,0:T(8,128)} %collective-permute-done.16.refs_2_, ...), custom_call_target="tpu_custom_call", output_to_operand_aliasing={{0}: (6, {}), {1}: (7, {})} | custom-call | flops 20000000000 | bytes 20000000 | tf_op jit(solution)/shard_map/front1/pallas_call | solution.py:313
  143.8 2.5 %collective-permute-start.20 = (f32[128,640]{1,0:T(8,128)}, f32[128,640]{1,0:T(8,128)S(1)}, u32[]{:S(2)}, u32[]{:S(2)}) collective-permute-start(f32[128,640]{1,0:T(8,128)} %get-tuple-element.59), channel_id=1, source_target_pairs={{0,16},{4,20},{8,24},{12,28},{16,0},{20,4},{24,8},{28,12},{32,48},... | collective-permute-start | bytes 983048 | tf_op jit(solution)/shard_map/ppermute | solution.py:371
  146.4 8.5 %collective-permute-done.20.refs_4_ = f32[128,640]{1,0:T(8,128)S(1)} collective-permute-done((f32[128,640]{1,0:T(8,128)}, f32[128,640]{1,0:T(8,128)S(1)}, u32[]{:S(2)}, u32[]{:S(2)}) %collective-permute-start.20) | collective-permute-done | bytes 327712 | tf_op jit(solution)/shard_map/ppermute | solution.py:371
  158.5 35.4 %front2.1 = (f32[3,256,1024]{2,1,0:T(8,128)}, f32[3,128,1024]{2,1,0:T(8,128)}, f32[128,512]{1,0:T(8,128)}) custom-call(s32[10]{0:T(128)} %add_add_fusion.1.refs_0_, f32[4,128,1152]{2,1,0:T(8,128)} %bitcast.16, f32[4,128,1152]{2,1,0:T(8,128)} %copy-done.6, f32[2,128,640]{2,1,0:T(8,128)} %get-tuple-element.58.refs_3_, ...), custom_call_target="tpu_custom_call", output_to_operand_aliasing={{0}: (6, {}), {1}: (7, {})} | custom-call | flops 20000000000 | bytes 20000000 | tf_op jit(solution)/shard_map/front2/pallas_call | solution.py:313
  (73 shorter events, 13.8 us)
Async XLA Ops:
  7.2 85.7 %all-gather.5.cloned.1.call-start = ((), (), s32[]{:S(2)}) async-start(), calls=%async_computation | async-start | bytes 2949120 | tf_op jit(solution)/shard_map/all_gather | solution.py:405
  12.5 3.1 %collective-permute-start = (f32[128,1152]{1,0:T(8,128)S(1)}, f32[128,1152]{1,0:T(8,128)S(1)}, u32[]{:S(2)}, u32[]{:S(2)}) collective-permute-start(f32[128,1152]{1,0:T(8,128)S(1)} %get-tuple-element.35), channel_id=1, source_target_pairs={{0,4},{4,0},{8,12},{12,8},{16,20},{20,16},{24,28},{28,24},{32,36},... | collective-permute-start | bytes 1769480 | tf_op jit(solution)/shard_map/ppermute | solution.py:371
  14.0 5.5 %collective-permute-start.8 = (f32[128,1152]{1,0:T(8,128)S(1)}, f32[128,1152]{1,0:T(8,128)S(1)}, u32[]{:S(2)}, u32[]{:S(2)}) collective-permute-start(f32[128,1152]{1,0:T(8,128)S(1)} %get-tuple-element.38), channel_id=1, source_target_pairs={{0,4},{4,0},{8,12},{12,8},{16,20},{20,16},{24,28},{28,24},{32,36},... | collective-permute-start | bytes 1769480 | tf_op jit(solution)/shard_map/ppermute | solution.py:371
  15.8 20.0 %collective-permute-start.1 = (f32[128,1536]{1,0:T(8,128)S(1)}, f32[128,1536]{1,0:T(8,128)S(1)}, u32[]{:S(2)}, u32[]{:S(2)}) collective-permute-start(f32[128,1536]{1,0:T(8,128)S(1)} %pad_maximum_fusion.refs_1_), channel_id=1, source_target_pairs={{0,1},{1,2},{2,3},{3,0},{4,5},{5,6},{6,7},{7,4},{8,9},{9,10},{10,1... | collective-permute-start | bytes 2359304 | tf_op jit(solution)/shard_map/ppermute | solution.py:376
  17.1 19.9 %collective-permute-start.3 = (f32[128,1536]{1,0:T(8,128)S(1)}, f32[128,1536]{1,0:T(8,128)}, u32[]{:S(2)}, u32[]{:S(2)}) collective-permute-start(f32[128,1536]{1,0:T(8,128)S(1)} %pad_maximum_fusion.refs_1_), channel_id=1, source_target_pairs={{0,3},{1,0},{2,1},{3,2},{4,7},{5,4},{6,5},{7,6},{8,11},{9,8},{10,9... | collective-permute-start | bytes 2359304 | tf_op jit(solution)/shard_map/ppermute | solution.py:376
  18.5 19.8 %collective-permute-start.10 = (f32[128,1152]{1,0:T(8,128)S(1)}, f32[128,1152]{1,0:T(8,128)S(1)}, u32[]{:S(2)}, u32[]{:S(2)}) collective-permute-start(f32[128,1152]{1,0:T(8,128)S(1)} %get-tuple-element.40), channel_id=1, source_target_pairs={{0,4},{4,0},{8,12},{12,8},{16,20},{20,16},{24,28},{28,24},{32,36},... | collective-permute-start | bytes 1769480 | tf_op jit(solution)/shard_map/ppermute | solution.py:371
  19.5 20.0 %collective-permute-start.9 = (f32[128,1152]{1,0:T(8,128)S(1)}, f32[128,1152]{1,0:T(8,128)S(1)}, u32[]{:S(2)}, u32[]{:S(2)}) collective-permute-start(f32[128,1152]{1,0:T(8,128)S(1)} %add.48), channel_id=1, source_target_pairs={{0,8},{4,12},{8,0},{12,4},{16,24},{20,28},{24,16},{28,20},{32,40},... | collective-permute-start | bytes 1769480 | tf_op jit(solution)/shard_map/ppermute | solution.py:371
  21.0 21.1 %collective-permute-start.5 = (f32[128,1536]{1,0:T(8,128)S(1)}, f32[128,1536]{1,0:T(8,128)}, u32[]{:S(2)}, u32[]{:S(2)}) collective-permute-start(f32[128,1536]{1,0:T(8,128)S(1)} %pad_maximum_fusion.refs_1_), channel_id=1, source_target_pairs={{0,4},{4,0},{8,12},{12,8},{16,20},{20,16},{24,28},{28,24},{32,36},... | collective-permute-start | bytes 2359304 | tf_op jit(solution)/shard_map/ppermute | solution.py:371
  35.8 14.3 %collective-permute-start.6 = (f32[128,1536]{1,0:T(8,128)S(1)}, f32[128,1536]{1,0:T(8,128)}, u32[]{:S(2)}, u32[]{:S(2)}) collective-permute-start(f32[128,1536]{1,0:T(8,128)S(1)} %collective-permute-done.1.refs_2_), channel_id=1, source_target_pairs={{0,4},{4,0},{8,12},{12,8},{16,20},{20,16},{24,28},{28,24},{32,36},... | collective-permute-start | bytes 2359304 | tf_op jit(solution)/shard_map/ppermute | solution.py:371
  37.0 13.1 %collective-permute-start.7 = (f32[128,1536]{1,0:T(8,128)}, f32[128,1536]{1,0:T(8,128)}, u32[]{:S(2)}, u32[]{:S(2)}) collective-permute-start(f32[128,1536]{1,0:T(8,128)} %collective-permute-done.3.refs_3_), channel_id=1, source_target_pairs={{0,4},{4,0},{8,12},{12,8},{16,20},{20,16},{24,28},{28,24},{32,36},... | collective-permute-start | bytes 2359304 | tf_op jit(solution)/shard_map/ppermute | solution.py:371
  38.3 11.7 %collective-permute-start.2 = (f32[64,1536]{1,0:T(8,128)S(1)}, f32[64,1536]{1,0:T(8,128)S(1)}, u32[]{:S(2)}, u32[]{:S(2)}) collective-permute-start(f32[64,1536]{1,0:T(8,128)S(1)} %slice.23), channel_id=1, source_target_pairs={{0,1},{1,2},{2,3},{3,0},{4,5},{5,6},{6,7},{7,4},{8,9},{9,10},{10,1... | collective-permute-start | bytes 1179656 | tf_op jit(solution)/shard_map/ppermute | solution.py:376
  39.5 10.5 %collective-permute-start.4 = (f32[64,1536]{1,0:T(8,128)S(1)}, f32[64,1536]{1,0:T(8,128)}, u32[]{:S(2)}, u32[]{:S(2)}) collective-permute-start(f32[64,1536]{1,0:T(8,128)S(1)} %slice.24), channel_id=1, source_target_pairs={{0,3},{1,0},{2,1},{3,2},{4,7},{5,4},{6,5},{7,6},{8,11},{9,8},{10,9... | collective-permute-start | bytes 1179656 | tf_op jit(solution)/shard_map/ppermute | solution.py:376
  50.1 93.3 %all-gather.7.cloned.1.call-start = ((), (), s32[]{:S(2)}) async-start(), calls=%async_computation.1 | async-start | bytes 2949120 | tf_op jit(solution)/shard_map/all_gather | solution.py:418
  50.2 6.1 %collective-permute-start.11 = (f32[64,1536]{1,0:T(8,128)S(1)}, f32[64,1536]{1,0:T(8,128)S(1)}, u32[]{:S(2)}, u32[]{:S(2)}) collective-permute-start(f32[64,1536]{1,0:T(8,128)S(1)} %collective-permute-done.2.refs_4_), channel_id=1, source_target_pairs={{0,4},{4,0},{8,12},{12,8},{16,20},{20,16},{24,28},{28,24},{32,36},... | collective-permute-start | bytes 1179656 | tf_op jit(solution)/shard_map/ppermute | solution.py:371
  51.3 4.9 %collective-permute-start.12 = (f32[64,1536]{1,0:T(8,128)}, f32[64,1536]{1,0:T(8,128)}, u32[]{:S(2)}, u32[]{:S(2)}) collective-permute-start(f32[64,1536]{1,0:T(8,128)} %collective-permute-done.4.refs_5_), channel_id=1, source_target_pairs={{0,4},{4,0},{8,12},{12,8},{16,20},{20,16},{24,28},{28,24},{32,36},... | collective-permute-start | bytes 1179656 | tf_op jit(solution)/shard_map/ppermute | solution.py:371
  52.3 41.9 %collective-permute-start.13 = (f32[128,1152]{1,0:T(8,128)S(1)}, f32[128,1152]{1,0:T(8,128)S(1)}, u32[]{:S(2)}, u32[]{:S(2)}) collective-permute-start(f32[128,1152]{1,0:T(8,128)S(1)} %add.50), channel_id=1, source_target_pairs={{0,8},{4,12},{8,0},{12,4},{16,24},{20,28},{24,16},{28,20},{32,40},... | collective-permute-start | bytes 1769480 | tf_op jit(solution)/shard_map/ppermute | solution.py:380
  53.6 40.6 %collective-permute-start.14 = (f32[128,1152]{1,0:T(8,128)S(1)}, f32[128,1152]{1,0:T(8,128)S(1)}, u32[]{:S(2)}, u32[]{:S(2)}) collective-permute-start(f32[128,1152]{1,0:T(8,128)S(1)} %add.50), channel_id=1, source_target_pairs={{0,16},{4,20},{8,24},{12,28},{16,0},{20,4},{24,8},{28,12},{32,48},... | collective-permute-start | bytes 1769480 | tf_op jit(solution)/shard_map/ppermute | solution.py:380
  56.2 37.9 %collective-permute-start.15 = (f32[128,1152]{1,0:T(8,128)S(1)}, f32[128,1152]{1,0:T(8,128)S(1)}, u32[]{:S(2)}, u32[]{:S(2)}) collective-permute-start(f32[128,1152]{1,0:T(8,128)S(1)} %add.50), channel_id=1, source_target_pairs={{0,24},{4,28},{8,16},{12,20},{16,8},{20,12},{24,0},{28,4},{32,56},... | collective-permute-start | bytes 1769480 | tf_op jit(solution)/shard_map/ppermute | solution.py:380
  92.9 13.9 %collective-permute-start.16 = (f32[4,128,1152]{2,1,0:T(8,128)}, f32[4,128,1152]{2,1,0:T(8,128)}, u32[]{:S(2)}, u32[]{:S(2)}) collective-permute-start(f32[4,128,1152]{2,1,0:T(8,128)} %bitcast.13), channel_id=1, source_target_pairs={{0,4},{4,0},{8,12},{12,8},{16,20},{20,16},{24,28},{28,24},{32,36},... | collective-permute-start | bytes 7077896 | tf_op jit(solution)/shard_map/ppermute | solution.py:371
  95.3 9.4 %collective-permute-start.17 = (f32[128,640]{1,0:T(8,128)S(1)}, f32[128,640]{1,0:T(8,128)S(1)}, u32[]{:S(2)}, u32[]{:S(2)}) collective-permute-start(f32[128,640]{1,0:T(8,128)S(1)} %copy-done.10), channel_id=1, source_target_pairs={{0,8},{4,12},{8,0},{12,4},{16,24},{20,28},{24,16},{28,20},{32,40},... | collective-permute-start | bytes 983048 | tf_op jit(solution)/shard_map/ppermute | solution.py:371
  104.7 2.1 %collective-permute-start.18 = (f32[128,640]{1,0:T(8,128)S(1)}, f32[128,640]{1,0:T(8,128)S(1)}, u32[]{:S(2)}, u32[]{:S(2)}) collective-permute-start(f32[128,640]{1,0:T(8,128)S(1)} %collective-permute-done.17.refs_4_), channel_id=1, source_target_pairs={{0,4},{4,0},{8,12},{12,8},{16,20},{20,16},{24,28},{28,24},{32,36},... | collective-permute-start | bytes 983048 | tf_op jit(solution)/shard_map/ppermute | solution.py:371
  143.4 13.6 %collective-permute-start.19 = (f32[4,128,1152]{2,1,0:T(8,128)}, f32[4,128,1152]{2,1,0:T(8,128)S(1)}, u32[]{:S(2)}, u32[]{:S(2)}) collective-permute-start(f32[4,128,1152]{2,1,0:T(8,128)} %bitcast.15), channel_id=1, source_target_pairs={{0,4},{4,0},{8,12},{12,8},{16,20},{20,16},{24,28},{28,24},{32,36},... | collective-permute-start | bytes 7077896 | tf_op jit(solution)/shard_map/ppermute | solution.py:371
  143.8 11.0 %collective-permute-start.20 = (f32[128,640]{1,0:T(8,128)}, f32[128,640]{1,0:T(8,128)S(1)}, u32[]{:S(2)}, u32[]{:S(2)}) collective-permute-start(f32[128,640]{1,0:T(8,128)} %get-tuple-element.59), channel_id=1, source_target_pairs={{0,16},{4,20},{8,24},{12,28},{16,0},{20,4},{24,8},{28,12},{32,48},... | collective-permute-start | bytes 983048 | tf_op jit(solution)/shard_map/ppermute | solution.py:371
  154.9 2.1 %collective-permute-start.21 = (f32[128,640]{1,0:T(8,128)S(1)}, f32[128,640]{1,0:T(8,128)S(1)}, u32[]{:S(2)}, u32[]{:S(2)}) collective-permute-start(f32[128,640]{1,0:T(8,128)S(1)} %collective-permute-done.20.refs_4_), channel_id=1, source_target_pairs={{0,4},{4,0},{8,12},{12,8},{16,20},{20,16},{24,28},{28,24},{32,36},... | collective-permute-start | bytes 983048 | tf_op jit(solution)/shard_map/ppermute | solution.py:371
  (14 other events, 66.8 us)
Sparse Core Ops, SparseCore 0:
  50.2 35.9 all-gather.4
  95.4 34.8 all-gather.6

commit v2 on v1

--- a/solution.py
+++ b/solution.py
@@ -266,8 +266,11 @@
         E[...] = F[blk(nxt), blk(nxt)] - nt4(near, near)
         W = jnp.concatenate(block_inverse([D[8 * g : 8 * g + 8, :] for g in range(BLK // 8)]), axis=0)
         WW[...] = stack_split(W)
-        l = stack_split(nt4(stack_split(T[blk(nxt), :]), WW[...]))
-        D[...] = E[...] - nt4(l, l)
+        wh, wl = split(W)
+        th, tl = split(T[blk(nxt), :])
+        v = nt(jnp.concatenate([th, th, tl], axis=1), jnp.concatenate([wh, wl, wh], axis=1))
+        h, l = split(v)
+        D[...] = E[...] - nt(jnp.concatenate([h, h, l], axis=1), jnp.concatenate([h, l, h], axis=1))
 
     lax.fori_loop(0, 4, lambda k, c: (step(k, 0, 384), c)[1], 0)
     lax.fori_loop(4, 8, lambda k, c: (step(k, 384, 896), c)[1], 0)
@@ -333,7 +336,7 @@
             pltpu.VMEM((2, BLK, 640), f32),
             pltpu.SemaphoreType.DMA((40,)),
         ],
-        compiler_params=pltpu.CompilerParams(vmem_limit_bytes=60 << 20),
+        compiler_params=pltpu.CompilerParams(vmem_limit_bytes=63 << 20),
         cost_estimate=pl.CostEstimate(flops=20_000_000_000, transcendentals=0, bytes_accessed=20_000_000),
         name=f"front{level}",
     )(ids, *inputs)

time: 201 us -> 201 us (level)
    unnamed x28 -> x20, local copies, waits for them, and re-layouts: 7.23 us -> 5.71 us
  transfers between devices with their start and end apart: 24 -> 24, of which waited for: 8 -> 8; matrix products, arithmetic and copies ran while one was open for 3% -> 4% of each run, Pallas kernels for 36% -> 35%
where the time goes in v2:
time: 201 us
  Pallas kernels  107 us (53%)
  waiting for transfers between devices  42.9 us (21%)
  starting transfers between devices  22.6 us (11%)
  between operations  14.2 us (7%)
  local copies, waits for them, and re-layouts  8.2 us (4%)
  other arithmetic  5.47 us (3%)
    pallas_call x3, Pallas kernels, front(): pl.pallas_call(lambda *refs: front_body(level, refs), in_specs=[smem] + [...  107 us
    ppermute x4, waiting for transfers between devices, shift(): return lax.ppermute(x, 'rows', [(i, (i + by) % size) for i in range(size)])  22.7 us
    ppermute x15, waiting for transfers between devices, swap(): lax.ppermute(x, 'leaf', [(i, i ^ 1 << stride) for i in range(lax.axis_siz...  20.1 us
    ppermute x15, starting transfers between devices, swap(): lax.ppermute(x, 'leaf', [(i, i ^ 1 << stride) for i in range(lax.axis_siz...  13.1 us
    unnamed x20, local copies, waits for them, and re-layouts  5.71 us
    ppermute x4, starting transfers between devices, shift(): return lax.ppermute(x, 'rows', [(i, (i + by) % size) for i in range(size)])  5.5 us
  transfers between devices with their start and end apart: 24, of which 8 were waited for; matrix products, arithmetic and copies ran while one was open for 4% of the time, Pallas kernels for 35%

profile of v2, /device:TPU:1, one launch (start us, length us, event | category | flops | bytes accessed | tf_op | source)
XLA Modules:
  0.0 200.8 jit_solution(18222108715850359927)
XLA Ops:
  7.3 1.9 copy-done
  9.2 1.4 copy-done.1
  12.5 1.5 collective-permute-start
  14.1 1.5 collective-permute-done
  15.8 1.4 collective-permute-start.1
  17.1 1.4 collective-permute-start.3
  19.5 1.5 collective-permute-start.9
  21.2 14.6 %collective-permute-done.1.refs_2_ = f32[128,1536]{1,0:T(8,128)} collective-permute-done((f32[128,1536]{1,0:T(8,128)S(1)}, f32[128,1536]{1,0:T(8,128)}, u32[]{:S(2)}, u32[]{:S(2)}) %collective-permute-start.1) | collective-permute-done | bytes 786464 | tf_op jit(solution)/shard_map/ppermute | solution.py:379
  35.9 1.2 collective-permute-start.6
  38.2 1.0 slice.24
  39.3 1.3 collective-permute-start.2
  40.5 1.5 collective-permute-start.4
  43.0 7.9 %collective-permute-done.2.refs_4_ = f32[64,1536]{1,0:T(8,128)} collective-permute-done((f32[64,1536]{1,0:T(8,128)S(1)}, f32[64,1536]{1,0:T(8,128)}, u32[]{:S(2)}, u32[]{:S(2)}) %collective-permute-start.2) | collective-permute-done | bytes 393248 | tf_op jit(solution)/shard_map/ppermute | solution.py:379
  51.2 1.2 collective-permute-start.11
  53.2 1.3 collective-permute-start.13
  54.5 2.6 %collective-permute-start.14 = (f32[128,1152]{1,0:T(8,128)S(1)}, f32[128,1152]{1,0:T(8,128)}, u32[]{:S(2)}, u32[]{:S(2)}) collective-permute-start(f32[128,1152]{1,0:T(8,128)S(1)} %add.50), channel_id=1, source_target_pairs={{0,16},{4,20},{8,24},{12,28},{16,0},{20,4},{24,8},{28,12},{32,48},... | collective-permute-start | bytes 1769480 | tf_op jit(solution)/shard_map/ppermute | solution.py:383
  57.2 35.6 %front0.1 = (f32[3,256,1024]{2,1,0:T(8,128)}, f32[3,128,1024]{2,1,0:T(8,128)}, f32[2,128,640]{2,1,0:T(8,128)}, f32[128,640]{1,0:T(8,128)}) custom-call(s32[10]{0:T(128)} %add_add_fusion.2.refs_0_, f32[128,1536]{1,0:T(8,128)} %copy-done.3, f32[128,1536]{1,0:T(8,128)} %collective-permute-done.1.refs_2_, f32[128,1536]{1,0:T(8,128)} %collective-permute-done.3.refs_3_, ...), custom_call_target="tpu_custom_call" | custom-call | flops 20000000000 | bytes 20000000 | tf_op jit(solution)/shard_map/front0/pallas_call | solution.py:316
  92.8 1.3 collective-permute-start.16
  94.1 2.4 %add_add_fusion = f32[128,1152]{1,0:T(8,128)} fusion(f32[128,1152]{1,0:T(8,128)} %collective-permute-done.15, f32[128,1152]{1,0:T(8,128)} %collective-permute-done.14, f32[128,1152]{1,0:T(8,128)S(1)} %add.50, f32[128,1152]{1,0:T(8,128)} %collective-permute-done.13), kind=kLoop, calls=%fused_computation.1 | loop fusion | flops 442368 | bytes 2949120 | tf_op jit(solution)/shard_map/add | solution.py:421
  96.7 9.2 %collective-permute-done.17.refs_4_ = f32[128,640]{1,0:T(8,128)S(1)} collective-permute-done((f32[128,640]{1,0:T(8,128)S(1)}, f32[128,640]{1,0:T(8,128)S(1)}, u32[]{:S(2)}, u32[]{:S(2)}) %collective-permute-start.17) | collective-permute-done | bytes 327712 | tf_op jit(solution)/shard_map/ppermute | solution.py:374
  108.7 35.6 %front1.1 = (f32[3,256,1024]{2,1,0:T(8,128)}, f32[3,128,1024]{2,1,0:T(8,128)}, f32[2,128,640]{2,1,0:T(8,128)}, f32[128,640]{1,0:T(8,128)}) custom-call(s32[10]{0:T(128)} %add_add_fusion.3.refs_0_, f32[4,128,1152]{2,1,0:T(8,128)} %bitcast.14, f32[4,128,1152]{2,1,0:T(8,128)} %collective-permute-done.16.refs_2_, ...), custom_call_target="tpu_custom_call", output_to_operand_aliasing={{0}: (6, {}), {1}: (7, {})} | custom-call | flops 20000000000 | bytes 20000000 | tf_op jit(solution)/shard_map/front1/pallas_call | solution.py:316
  144.8 2.6 %collective-permute-start.20 = (f32[128,640]{1,0:T(8,128)}, f32[128,640]{1,0:T(8,128)S(1)}, u32[]{:S(2)}, u32[]{:S(2)}) collective-permute-start(f32[128,640]{1,0:T(8,128)} %get-tuple-element.59), channel_id=1, source_target_pairs={{0,16},{4,20},{8,24},{12,28},{16,0},{20,4},{24,8},{28,12},{32,48},... | collective-permute-start | bytes 983048 | tf_op jit(solution)/shard_map/ppermute | solution.py:374
  147.4 8.3 %collective-permute-done.20.refs_4_ = f32[128,640]{1,0:T(8,128)S(1)} collective-permute-done((f32[128,640]{1,0:T(8,128)}, f32[128,640]{1,0:T(8,128)S(1)}, u32[]{:S(2)}, u32[]{:S(2)}) %collective-permute-start.20) | collective-permute-done | bytes 327712 | tf_op jit(solution)/shard_map/ppermute | solution.py:374
  158.7 35.2 %front2.1 = (f32[3,256,1024]{2,1,0:T(8,128)}, f32[3,128,1024]{2,1,0:T(8,128)}, f32[128,512]{1,0:T(8,128)}) custom-call(s32[10]{0:T(128)} %add_add_fusion.1.refs_0_, f32[4,128,1152]{2,1,0:T(8,128)} %bitcast.16, f32[4,128,1152]{2,1,0:T(8,128)} %collective-permute-done.19.refs_2_, ...), custom_call_target="tpu_custom_call", output_to_operand_aliasing={{0}: (6, {}), {1}: (7, {})} | custom-call | flops 20000000000 | bytes 20000000 | tf_op jit(solution)/shard_map/front2/pallas_call | solution.py:316
  (65 shorter events, 13.2 us)
Async XLA Ops:
  7.2 85.7 %all-gather.5.cloned.1.call-start = ((), (), s32[]{:S(2)}) async-start(), calls=%async_computation | async-start | bytes 2949120 | tf_op jit(solution)/shard_map/all_gather | solution.py:408
  12.5 3.1 %collective-permute-start = (f32[128,1152]{1,0:T(8,128)S(1)}, f32[128,1152]{1,0:T(8,128)S(1)}, u32[]{:S(2)}, u32[]{:S(2)}) collective-permute-start(f32[128,1152]{1,0:T(8,128)S(1)} %get-tuple-element.35), channel_id=1, source_target_pairs={{0,4},{4,0},{8,12},{12,8},{16,20},{20,16},{24,28},{28,24},{32,36},... | collective-permute-start | bytes 1769480 | tf_op jit(solution)/shard_map/ppermute | solution.py:374
  14.0 5.5 %collective-permute-start.8 = (f32[128,1152]{1,0:T(8,128)S(1)}, f32[128,1152]{1,0:T(8,128)S(1)}, u32[]{:S(2)}, u32[]{:S(2)}) collective-permute-start(f32[128,1152]{1,0:T(8,128)S(1)} %get-tuple-element.38), channel_id=1, source_target_pairs={{0,4},{4,0},{8,12},{12,8},{16,20},{20,16},{24,28},{28,24},{32,36},... | collective-permute-start | bytes 1769480 | tf_op jit(solution)/shard_map/ppermute | solution.py:374
  15.8 20.1 %collective-permute-start.1 = (f32[128,1536]{1,0:T(8,128)S(1)}, f32[128,1536]{1,0:T(8,128)}, u32[]{:S(2)}, u32[]{:S(2)}) collective-permute-start(f32[128,1536]{1,0:T(8,128)S(1)} %pad_maximum_fusion.refs_1_), channel_id=1, source_target_pairs={{0,1},{1,2},{2,3},{3,0},{4,5},{5,6},{6,7},{7,4},{8,9},{9,10},{10,1... | collective-permute-start | bytes 2359304 | tf_op jit(solution)/shard_map/ppermute | solution.py:379
  17.1 20.0 %collective-permute-start.3 = (f32[128,1536]{1,0:T(8,128)S(1)}, f32[128,1536]{1,0:T(8,128)}, u32[]{:S(2)}, u32[]{:S(2)}) collective-permute-start(f32[128,1536]{1,0:T(8,128)S(1)} %pad_maximum_fusion.refs_1_), channel_id=1, source_target_pairs={{0,3},{1,0},{2,1},{3,2},{4,7},{5,4},{6,5},{7,6},{8,11},{9,8},{10,9... | collective-permute-start | bytes 2359304 | tf_op jit(solution)/shard_map/ppermute | solution.py:379
  18.5 20.8 %collective-permute-start.10 = (f32[128,1152]{1,0:T(8,128)S(1)}, f32[128,1152]{1,0:T(8,128)S(1)}, u32[]{:S(2)}, u32[]{:S(2)}) collective-permute-start(f32[128,1152]{1,0:T(8,128)S(1)} %get-tuple-element.40), channel_id=1, source_target_pairs={{0,4},{4,0},{8,12},{12,8},{16,20},{20,16},{24,28},{28,24},{32,36},... | collective-permute-start | bytes 1769480 | tf_op jit(solution)/shard_map/ppermute | solution.py:374
  19.5 21.0 %collective-permute-start.9 = (f32[128,1152]{1,0:T(8,128)S(1)}, f32[128,1152]{1,0:T(8,128)S(1)}, u32[]{:S(2)}, u32[]{:S(2)}) collective-permute-start(f32[128,1152]{1,0:T(8,128)S(1)} %add.48), channel_id=1, source_target_pairs={{0,8},{4,12},{8,0},{12,4},{16,24},{20,28},{24,16},{28,20},{32,40},... | collective-permute-start | bytes 1769480 | tf_op jit(solution)/shard_map/ppermute | solution.py:374
  21.0 22.1 %collective-permute-start.5 = (f32[128,1536]{1,0:T(8,128)S(1)}, f32[128,1536]{1,0:T(8,128)}, u32[]{:S(2)}, u32[]{:S(2)}) collective-permute-start(f32[128,1536]{1,0:T(8,128)S(1)} %pad_maximum_fusion.refs_1_), channel_id=1, source_target_pairs={{0,4},{4,0},{8,12},{12,8},{16,20},{20,16},{24,28},{28,24},{32,36},... | collective-permute-start | bytes 2359304 | tf_op jit(solution)/shard_map/ppermute | solution.py:374
  35.9 15.2 %collective-permute-start.6 = (f32[128,1536]{1,0:T(8,128)}, f32[128,1536]{1,0:T(8,128)}, u32[]{:S(2)}, u32[]{:S(2)}) collective-permute-start(f32[128,1536]{1,0:T(8,128)} %collective-permute-done.1.refs_2_), channel_id=1, source_target_pairs={{0,4},{4,0},{8,12},{12,8},{16,20},{20,16},{24,28},{28,24},{32,36},... | collective-permute-start | bytes 2359304 | tf_op jit(solution)/shard_map/ppermute | solution.py:374
  37.1 14.0 %collective-permute-start.7 = (f32[128,1536]{1,0:T(8,128)}, f32[128,1536]{1,0:T(8,128)}, u32[]{:S(2)}, u32[]{:S(2)}) collective-permute-start(f32[128,1536]{1,0:T(8,128)} %collective-permute-done.3.refs_3_), channel_id=1, source_target_pairs={{0,4},{4,0},{8,12},{12,8},{16,20},{20,16},{24,28},{28,24},{32,36},... | collective-permute-start | bytes 2359304 | tf_op jit(solution)/shard_map/ppermute | solution.py:374
  39.3 11.6 %collective-permute-start.2 = (f32[64,1536]{1,0:T(8,128)S(1)}, f32[64,1536]{1,0:T(8,128)}, u32[]{:S(2)}, u32[]{:S(2)}) collective-permute-start(f32[64,1536]{1,0:T(8,128)S(1)} %slice.23), channel_id=1, source_target_pairs={{0,1},{1,2},{2,3},{3,0},{4,5},{5,6},{6,7},{7,4},{8,9},{9,10},{10,1... | collective-permute-start | bytes 1179656 | tf_op jit(solution)/shard_map/ppermute | solution.py:379
  40.5 10.5 %collective-permute-start.4 = (f32[64,1536]{1,0:T(8,128)S(1)}, f32[64,1536]{1,0:T(8,128)}, u32[]{:S(2)}, u32[]{:S(2)}) collective-permute-start(f32[64,1536]{1,0:T(8,128)S(1)} %slice.24), channel_id=1, source_target_pairs={{0,3},{1,0},{2,1},{3,2},{4,7},{5,4},{6,5},{7,6},{8,11},{9,8},{10,9... | collective-permute-start | bytes 1179656 | tf_op jit(solution)/shard_map/ppermute | solution.py:379
  51.1 93.2 %all-gather.7.cloned.1.call-start = ((), (), s32[]{:S(2)}) async-start(), calls=%async_computation.1 | async-start | bytes 2949120 | tf_op jit(solution)/shard_map/all_gather | solution.py:421
  51.2 6.0 %collective-permute-start.11 = (f32[64,1536]{1,0:T(8,128)}, f32[64,1536]{1,0:T(8,128)}, u32[]{:S(2)}, u32[]{:S(2)}) collective-permute-start(f32[64,1536]{1,0:T(8,128)} %collective-permute-done.2.refs_4_), channel_id=1, source_target_pairs={{0,4},{4,0},{8,12},{12,8},{16,20},{20,16},{24,28},{28,24},{32,36},... | collective-permute-start | bytes 1179656 | tf_op jit(solution)/shard_map/ppermute | solution.py:374
  52.3 4.8 %collective-permute-start.12 = (f32[64,1536]{1,0:T(8,128)}, f32[64,1536]{1,0:T(8,128)}, u32[]{:S(2)}, u32[]{:S(2)}) collective-permute-start(f32[64,1536]{1,0:T(8,128)} %collective-permute-done.4.refs_5_), channel_id=1, source_target_pairs={{0,4},{4,0},{8,12},{12,8},{16,20},{20,16},{24,28},{28,24},{32,36},... | collective-permute-start | bytes 1179656 | tf_op jit(solution)/shard_map/ppermute | solution.py:374
  53.2 40.9 %collective-permute-start.13 = (f32[128,1152]{1,0:T(8,128)S(1)}, f32[128,1152]{1,0:T(8,128)}, u32[]{:S(2)}, u32[]{:S(2)}) collective-permute-start(f32[128,1152]{1,0:T(8,128)S(1)} %add.50), channel_id=1, source_target_pairs={{0,8},{4,12},{8,0},{12,4},{16,24},{20,28},{24,16},{28,20},{32,40},... | collective-permute-start | bytes 1769480 | tf_op jit(solution)/shard_map/ppermute | solution.py:383
  54.5 39.6 %collective-permute-start.14 = (f32[128,1152]{1,0:T(8,128)S(1)}, f32[128,1152]{1,0:T(8,128)}, u32[]{:S(2)}, u32[]{:S(2)}) collective-permute-start(f32[128,1152]{1,0:T(8,128)S(1)} %add.50), channel_id=1, source_target_pairs={{0,16},{4,20},{8,24},{12,28},{16,0},{20,4},{24,8},{28,12},{32,48},... | collective-permute-start | bytes 1769480 | tf_op jit(solution)/shard_map/ppermute | solution.py:383
  57.2 37.0 %collective-permute-start.15 = (f32[128,1152]{1,0:T(8,128)S(1)}, f32[128,1152]{1,0:T(8,128)}, u32[]{:S(2)}, u32[]{:S(2)}) collective-permute-start(f32[128,1152]{1,0:T(8,128)S(1)} %add.50), channel_id=1, source_target_pairs={{0,24},{4,28},{8,16},{12,20},{16,8},{20,12},{24,0},{28,4},{32,56},... | collective-permute-start | bytes 1769480 | tf_op jit(solution)/shard_map/ppermute | solution.py:383
  92.8 15.1 %collective-permute-start.16 = (f32[4,128,1152]{2,1,0:T(8,128)}, f32[4,128,1152]{2,1,0:T(8,128)}, u32[]{:S(2)}, u32[]{:S(2)}) collective-permute-start(f32[4,128,1152]{2,1,0:T(8,128)} %bitcast.13), channel_id=1, source_target_pairs={{0,4},{4,0},{8,12},{12,8},{16,20},{20,16},{24,28},{28,24},{32,36},... | collective-permute-start | bytes 7077896 | tf_op jit(solution)/shard_map/ppermute | solution.py:374
  96.5 9.4 %collective-permute-start.17 = (f32[128,640]{1,0:T(8,128)S(1)}, f32[128,640]{1,0:T(8,128)S(1)}, u32[]{:S(2)}, u32[]{:S(2)}) collective-permute-start(f32[128,640]{1,0:T(8,128)S(1)} %copy-done.6), channel_id=1, source_target_pairs={{0,8},{4,12},{8,0},{12,4},{16,24},{20,28},{24,16},{28,20},{32,40},... | collective-permute-start | bytes 983048 | tf_op jit(solution)/shard_map/ppermute | solution.py:374
  105.9 2.1 %collective-permute-start.18 = (f32[128,640]{1,0:T(8,128)S(1)}, f32[128,640]{1,0:T(8,128)S(1)}, u32[]{:S(2)}, u32[]{:S(2)}) collective-permute-start(f32[128,640]{1,0:T(8,128)S(1)} %collective-permute-done.17.refs_4_), channel_id=1, source_target_pairs={{0,4},{4,0},{8,12},{12,8},{16,20},{20,16},{24,28},{28,24},{32,36},... | collective-permute-start | bytes 983048 | tf_op jit(solution)/shard_map/ppermute | solution.py:374
  144.4 13.6 %collective-permute-start.19 = (f32[4,128,1152]{2,1,0:T(8,128)}, f32[4,128,1152]{2,1,0:T(8,128)}, u32[]{:S(2)}, u32[]{:S(2)}) collective-permute-start(f32[4,128,1152]{2,1,0:T(8,128)} %bitcast.15), channel_id=1, source_target_pairs={{0,4},{4,0},{8,12},{12,8},{16,20},{20,16},{24,28},{28,24},{32,36},... | collective-permute-start | bytes 7077896 | tf_op jit(solution)/shard_map/ppermute | solution.py:374
  144.8 10.9 %collective-permute-start.20 = (f32[128,640]{1,0:T(8,128)}, f32[128,640]{1,0:T(8,128)S(1)}, u32[]{:S(2)}, u32[]{:S(2)}) collective-permute-start(f32[128,640]{1,0:T(8,128)} %get-tuple-element.59), channel_id=1, source_target_pairs={{0,16},{4,20},{8,24},{12,28},{16,0},{20,4},{24,8},{28,12},{32,48},... | collective-permute-start | bytes 983048 | tf_op jit(solution)/shard_map/ppermute | solution.py:374
  155.7 2.2 %collective-permute-start.21 = (f32[128,640]{1,0:T(8,128)S(1)}, f32[128,640]{1,0:T(8,128)S(1)}, u32[]{:S(2)}, u32[]{:S(2)}) collective-permute-start(f32[128,640]{1,0:T(8,128)S(1)} %collective-permute-done.20.refs_4_), channel_id=1, source_target_pairs={{0,4},{4,0},{8,12},{12,8},{16,20},{20,16},{24,28},{28,24},{32,36},... | collective-permute-start | bytes 983048 | tf_op jit(solution)/shard_map/ppermute | solution.py:374
  (10 other events, 54.3 us)
Sparse Core Ops, SparseCore 0:
  51.2 35.8 all-gather.4
  96.6 34.7 all-gather.6
